TPU v7x, 512 devices: a whole 4x4x16 slice. The times are simulated.
512 devices in a mesh: dp: 64 (over y, x, z_lo), mp: 8 (over z_hi, core).
Axes of the slice: x: 4, y: 4, z: 16 (z_hi: 4, z_lo: 4; z = z_hi * 4 + z_lo), core: 2. Of those that a mesh axis runs over, the one named last changes fastest.
Arguments:
- normed: bfloat16 [4096, 6144], P('mp', 'dp'), may hold values from -6 to 6
- hidden_cot: bfloat16 [4096, 12288], P('mp', 'dp'), may hold values from -6 to 6
- up_rows: bfloat16 [12288, 6144], P('dp'), may hold values from -0.078125 to 0.078125
Outputs:
- hidden: bfloat16 [4096, 12288], P('mp', 'dp')
- input_grad: bfloat16 [4096, 6144], P('mp', 'dp')
- up_grad: bfloat16 [12288, 6144], P('dp')
All inputs are finite; a program needn't handle non-finite values.
Results may differ from a plain program's by a relative error of at most 0.013.
Values may be sent and summed in bfloat16 or wider, within the bound.
No kernel may reach another device: no remote copies, remote signals or barrier semaphores. Data moves between devices by JAX's collectives and lax.ppermute only.
A program may use at most 64 MiB of HBM per device.

v0:
```python
import jax
import jax.numpy as jnp
from jax import lax
from jax.sharding import PartitionSpec as P

inv_sqrt_two = 0.7071067811865476
inv_sqrt_two_pi = 0.3989422804014327


def gelu_parts(preact):
    normal_cdf = 0.5 * (1.0 + lax.erf(preact * inv_sqrt_two))
    gelu_out = preact * normal_cdf
    gelu_slope = normal_cdf + preact * jnp.exp(-0.5 * preact * preact) * inv_sqrt_two_pi
    return (gelu_out, gelu_slope)


def contract_last(left, right):
    return lax.dot_general(
        left, right, (((1,), (1,)), ((), ())), preferred_element_type=jnp.float32
    )


def contract_first(left, right):
    return lax.dot_general(
        left, right, (((0,), (0,)), ((), ())), preferred_element_type=jnp.float32
    )


def local(normed, hidden_cot, up_rows):
    full_in = lax.all_gather(normed, "dp", axis=1, tiled=True)
    column_rows = lax.all_to_all(up_rows, "dp", split_axis=1, concat_axis=0, tiled=True)
    replicas = lax.axis_size("mp")
    preact = contract_last(full_in, up_rows)
    gelu_out, gelu_slope = gelu_parts(preact)
    hidden = gelu_out.astype(jnp.bfloat16)
    hidden_grad = (hidden_cot.astype(jnp.float32) * gelu_slope).astype(jnp.bfloat16)
    up_term = contract_first(hidden_grad, full_in)
    up_total = lax.psum(up_term.astype(jnp.bfloat16), "mp").astype(jnp.float32)
    up_grad = (up_total / replicas).astype(jnp.bfloat16)
    input_total = jnp.dot(
        lax.all_gather(hidden_grad, "dp", axis=1, tiled=True),
        column_rows,
        preferred_element_type=jnp.float32,
    )
    input_grad = input_total.astype(jnp.bfloat16)
    return (hidden, input_grad, up_grad)


def solution(mesh):
    return jax.shard_map(
        local,
        mesh=mesh,
        in_specs=(P("mp", "dp"), P("mp", "dp"), P("dp", None)),
        out_specs=(P("mp", "dp"), P("mp", "dp"), P("dp", None)),
        check_vma=False,
    )
```

profile of v0, /device:TPU:128, one launch (start us, length us, event | category | flops | bytes accessed | tf_op | source)
XLA Modules:
  0.0 975.7 jit_solution(11073580016380807391)
XLA Ops:
  7.2 0.0 all-gather.3.cloned.1.call-start
  7.2 0.7 all-gather.3.cloned.1.call-update
  7.9 0.0 all-reduce.2.cloned.1.call-start
  7.9 379.4 %all-gather.3.cloned.1.call-done = bf16[512,6144]{0,1:T(8,128)(2,1)} async-done(((bf16[512,96]{0,1:T(8,128)(2,1)}), bf16[512,6144]{0,1:T(8,128)(2,1)}) %all-gather.3.cloned.1.call-update) | async-done | bytes 6291472 | tf_op jit(solution)/shard_map/all_gather | solution.py:30
  387.4 5.7 fusion.5
  393.1 0.0 copy-start
  393.1 6.4 convolution_convert_fusion
  399.5 0.0 copy-done
  399.5 0.0 all-reduce.2.cloned.1.call-update
  399.5 0.0 all-gather.5.cloned.1.call-start
  399.6 0.7 all-gather.5.cloned.1.call-update
  400.3 3.0 copy.7
  403.3 95.6 %all_to_all.19 = bf16[192,64,96]{0,2,1:T(8,128)(2,1)S(1)} all-to-all(bf16[192,64,96]{0,2,1:T(8,128)(2,1)S(1)} %bitcast.11), channel_id=1, replica_groups=mesh['dp'=64,'mp'=8] {'dp'}, dimensions={1} | all-to-all | bytes 4718592 | tf_op jit(solution)/shard_map/all_to_all | solution.py:31
  498.8 3.4 copy.8
  502.3 5.1 all_to_all.17
  507.4 50.8 %all-reduce.2.cloned.1.call-done = bf16[192,6144]{1,0:T(8,128)(2,1)} async-done(((bf16[192,6144]{1,0:T(8,128)(2,1)}), bf16[192,6144]{1,0:T(8,128)(2,1)}) %all-reduce.2.cloned.1.call-update) | async-done | bytes 2359312 | tf_op jit(solution)/shard_map/psum | solution.py:38
  558.2 3.5 multiply_convert_fusion
  561.7 400.1 %all-gather.5.cloned.1.call-done = bf16[512,12288]{0,1:T(8,128)(2,1)} async-done(((bf16[512,192]{0,1:T(8,128)(2,1)}), bf16[512,12288]{0,1:T(8,128)(2,1)}) %all-gather.5.cloned.1.call-update) | async-done | bytes 12582928 | tf_op jit(solution)/shard_map/all_gather | solution.py:41
  961.8 7.3 convolution_convert_fusion.1
Async XLA Ops:
  7.2 380.2 %all-gather.3.cloned.1.call-start = ((), (), s32[]{:S(2)}) async-start(), calls=%async_computation.1 | async-start | bytes 6389760 | tf_op jit(solution)/shard_map/all_gather | solution.py:30
  7.9 550.3 %all-reduce.2.cloned.1.call-start = ((), (), s32[]{:S(2)}) async-start(), calls=%async_computation.3 | async-start | bytes 4718592 | tf_op jit(solution)/shard_map/psum | solution.py:38
  393.1 6.4 copy-start
  399.5 562.3 %all-gather.5.cloned.1.call-start = ((), (), s32[]{:S(2)}) async-start(), calls=%async_computation.2 | async-start | bytes 12779520 | tf_op jit(solution)/shard_map/all_gather | solution.py:41
Sparse Core Ops, SparseCore 0:
  10.0 377.2 all-gather.2
  399.6 158.5 all-reduce.1
  560.3 401.4 all-gather.4
where the time goes:
time: 976 us
  waiting for transfers between devices  832 us (85%)
  blocking collectives  95.6 us (10%)
  matrix products  19.5 us (2%)
  between operations  13.8 us (1%)
  local copies, waits for them, and re-layouts  11.6 us (1%)
    all_gather x1, waiting for transfers between devices, local(): lax.all_gather(hidden_grad, 'dp', axis=1, tiled=True)  400 us
    all_gather x1, waiting for transfers between devices, local(): full_in = lax.all_gather(normed, 'dp', axis=1, tiled=True)  379 us
    all_to_all x1, blocking collectives, local(): lax.all_to_all(up_rows, 'dp', split_axis=1, concat_axis=0, tiled=True)  95.6 us
    psum x1, waiting for transfers between devices, local(): up_total = lax.psum(up_term.astype(jnp.bfloat16), 'mp').astype(jnp.float32)  50.8 us
  transfers between devices with their start and end apart: 3, of which 3 were waited for; matrix products, arithmetic and copies ran while one was open for 1% of the time, Pallas kernels for 0%

commit v1 on v0

--- a/solution.py
+++ b/solution.py
@@ -38,7 +38,9 @@
     up_total = lax.psum(up_term.astype(jnp.bfloat16), "mp").astype(jnp.float32)
     up_grad = (up_total / replicas).astype(jnp.bfloat16)
     input_total = jnp.dot(
-        lax.all_gather(hidden_grad, "dp", axis=1, tiled=True),
+        jnp.concatenate(
+            lax.all_to_all(jnp.stack([hidden_grad] * lax.axis_size("dp")), "dp", 0, 0), axis=1
+        ),
         column_rows,
         preferred_element_type=jnp.float32,
     )

time: 976 us -> 758 us (0.78)
  the two profiles are of different devices: /device:TPU:128 before, /device:TPU:32 now
where the time goes in v1:
time: 758 us
  waiting for transfers between devices  688 us (91%)
  starting transfers between devices  22.9 us (3%)
  matrix products  19.4 us (3%)
  between operations  14.1 us (2%)
  local copies, waits for them, and re-layouts  10.5 us (1%)
    all_gather x1, waiting for transfers between devices, local(): full_in = lax.all_gather(normed, 'dp', axis=1, tiled=True)  370 us
    psum x1, waiting for transfers between devices, local(): up_total = lax.psum(up_term.astype(jnp.bfloat16), 'mp').astype(jnp.float32)  260 us
    all_to_all x1, waiting for transfers between devices, local(): lax.all_to_all(jnp.stack([hidden_grad] * lax.axis_size('dp')), 'dp', 0, 0)  56.9 us
  transfers between devices with their start and end apart: 4, of which 3 were waited for; matrix products, arithmetic and copies ran while one was open for 3% of the time, Pallas kernels for 0%

profile of v1, /device:TPU:32, one launch (start us, length us, event | category | flops | bytes accessed | tf_op | source)
XLA Modules:
  0.0 758.0 jit_solution(6204170049940441262)
XLA Ops:
  7.2 0.0 all-gather.2.cloned.1.call-start
  7.2 0.7 all-gather.2.cloned.1.call-update
  7.9 0.0 copy-start
  7.9 4.5 copy.6
  12.4 11.7 %all-to-all-start.1 = ((bf16[192,64,96]{0,2,1:T(8,128)(2,1)}), bf16[192,64,96]{0,2,1:T(8,128)(2,1)S(1)}, u32[]{:S(2)}, u32[]{:S(2)}) async-start(bf16[192,64,96]{0,2,1:T(8,128)(2,1)} %bitcast.23), calls=%async_computation.1 | async-start | bytes 6291456 | tf_op jit(solution)/shard_map/all_to_all | solution.py:31
  24.1 370.2 %all-gather.2.cloned.1.call-done = bf16[512,6144]{0,1:T(8,128)(2,1)} async-done(((bf16[512,96]{0,1:T(8,128)(2,1)}), bf16[512,6144]{0,1:T(8,128)(2,1)}) %all-gather.2.cloned.1.call-update) | async-done | bytes 6291472 | tf_op jit(solution)/shard_map/all_gather | solution.py:30
  394.3 0.0 copy-done
  394.3 5.7 fusion.18
  400.1 0.0 all-to-all-done.1
  400.1 6.0 stack.2
  406.1 11.2 %all-to-all-start = ((bf16[64,512,192]{1,2,0:T(8,128)(2,1)}), bf16[64,512,192]{1,2,0:T(8,128)(2,1)}, u32[]{:S(2)}, u32[]{:S(2)}) async-start(bf16[64,512,192]{1,2,0:T(8,128)(2,1)} %stack.2), calls=%async_computation | async-start | bytes 25165824 | tf_op jit(solution)/shard_map/all_to_all | solution.py:42
  417.2 0.0 all-reduce.2.cloned.1.call-start
  417.3 6.4 convolution_convert_fusion
  423.7 0.0 all-reduce.2.cloned.1.call-update
  423.7 259.6 %all-reduce.2.cloned.1.call-done = bf16[192,6144]{1,0:T(8,128)(2,1)} async-done(((bf16[192,6144]{1,0:T(8,128)(2,1)}), bf16[192,6144]{1,0:T(8,128)(2,1)}) %all-reduce.2.cloned.1.call-update) | async-done | bytes 2359312 | tf_op jit(solution)/shard_map/psum | solution.py:38
  683.3 3.5 multiply_convert_fusion
  686.9 56.9 %all-to-all-done = bf16[64,512,192]{1,2,0:T(8,128)(2,1)} async-done(((bf16[64,512,192]{1,2,0:T(8,128)(2,1)}), bf16[64,512,192]{1,2,0:T(8,128)(2,1)}, u32[]{:S(2)}, u32[]{:S(2)}) %all-to-all-start) | async-done | bytes 12582944 | tf_op jit(solution)/shard_map/all_to_all | solution.py:42
  743.8 7.4 fusion.8
Async XLA Ops:
  7.2 387.2 %all-gather.2.cloned.1.call-start = ((), (), s32[]{:S(2)}) async-start(), calls=%async_computation.2 | async-start | bytes 6389760 | tf_op jit(solution)/shard_map/all_gather | solution.py:30
  7.9 386.4 %copy-start = (bf16[512,192]{0,1:T(8,128)(2,1)S(1)}, bf16[512,192]{0,1:T(8,128)(2,1)}, u32[]{:S(2)}) copy-start(bf16[512,192]{0,1:T(8,128)(2,1)} %param.4) | copy-start | bytes 589828
  12.4 387.6 %all-to-all-start.1 = ((bf16[192,64,96]{0,2,1:T(8,128)(2,1)}), bf16[192,64,96]{0,2,1:T(8,128)(2,1)S(1)}, u32[]{:S(2)}, u32[]{:S(2)}) async-start(bf16[192,64,96]{0,2,1:T(8,128)(2,1)} %bitcast.23), calls=%async_computation.1 | async-start | bytes 6291456 | tf_op jit(solution)/shard_map/all_to_all | solution.py:31
  406.1 337.8 %all-to-all-start = ((bf16[64,512,192]{1,2,0:T(8,128)(2,1)}), bf16[64,512,192]{1,2,0:T(8,128)(2,1)}, u32[]{:S(2)}, u32[]{:S(2)}) async-start(bf16[64,512,192]{1,2,0:T(8,128)(2,1)} %stack.2), calls=%async_computation | async-start | bytes 25165824 | tf_op jit(solution)/shard_map/all_to_all | solution.py:42
  417.2 266.1 %all-reduce.2.cloned.1.call-start = ((), (), s32[]{:S(2)}) async-start(), calls=%async_computation.3 | async-start | bytes 4718592 | tf_op jit(solution)/shard_map/psum | solution.py:38
Sparse Core Ops, SparseCore 0:
  10.1 384.2 all-gather.1
  423.8 259.4 all-reduce.1
